TPU v7x, 512 devices: a whole 4x8x8 slice. The times are simulated.
512 devices in a mesh: row: 16 (over x, y_lo), col: 32 (over y_hi, z, core).
Axes of the slice: x: 4, y: 8 (y_hi: 2, y_lo: 4; y = y_hi * 4 + y_lo), z: 8, core: 2. Of those that a mesh axis runs over, the one named last changes fastest.
Arguments:
- bricks: bfloat16 [16, 32, 2, 16, 128, 128], P('row', 'col'), may hold values from -393216 to 393216
- brick_coords: int32 [16, 32, 3, 2], P('row', 'col'), may hold values from 0 to 31, as said below
- brick_counts: int32 [16, 32], P('row', 'col'), may hold values from 0 to 2, as said below
- step_sizes: float32 [2, 3], replicated, may hold values from 0.3 to 1
- init_a: float32 [16, 512, 256], P('row', 'col'), may hold values from -6 to 6
- init_b: float32 [32, 256, 256], P('col', 'row'), may hold values from -6 to 6
- init_c: float32 [512, 256], replicated, may hold values from -6 to 6
Outputs:
- factor_a: float32 [16, 512, 256], P('row', 'col')
- factor_b: float32 [32, 256, 256], P('col', 'row')
- factor_c: float32 [512, 256], replicated
Inputs may be any that keep to these rules, and one draw needn't show every extreme that they name: brick_counts of rows r and (r + half of the row axis) mod the row axis in one column add up to at most 3; some device holds 2 bricks. `brick_coords`: component 0 is below 4, component 1 below 2, component 2 below 32; dead slots hold arbitrary positions.
All inputs are finite; a program needn't handle non-finite values.
Results may differ from a plain program's by a relative error of at most 0.0003.
The roundings to bfloat16 on the way count: a program that leaves them out, or rounds other values in their place, can miss the bound.
Values may be sent and summed in bfloat16 or wider, within the bound.
No kernel may reach another device: no remote copies, remote signals or barrier semaphores. Data moves between devices by JAX's collectives and lax.ppermute only.
A program may use at most 64 MiB of HBM per device.

v0:
```python
import jax
import jax.numpy as jnp
from jax import lax
from jax.sharding import PartitionSpec as P


def brick_terms(brick, a_tile, b_tile, c_rows):
    depth, tile, _ = brick.shape
    wide = jnp.dot(
        brick.reshape(depth * tile, tile), b_tile, preferred_element_type=jnp.float32
    ).reshape(depth, tile, -1)
    c_wide = c_rows.astype(jnp.float32)[:, None, :]
    along_a = jnp.sum(wide * c_wide, axis=0)
    deep = jnp.einsum("kij,ir->kjr", brick, a_tile, preferred_element_type=jnp.float32)
    along_b = jnp.sum(deep * c_wide, axis=0)
    along_c = jnp.sum(deep * b_tile.astype(jnp.float32)[None, :, :], axis=1)
    return (along_a, along_b, along_c)


def add_tile(total, delta, start):
    old = lax.dynamic_slice_in_dim(total, start, delta.shape[0], 0)
    return lax.dynamic_update_slice_in_dim(total, old + delta, start, 0)


def gram(values):
    return jnp.dot(values.T, values, preferred_element_type=jnp.float32)


def project(state, hess, drive, rate):
    scale = jnp.sum(jnp.abs(hess), axis=1) + 1e-06
    slope = (
        jnp.dot(state, hess, precision=lax.Precision.HIGHEST, preferred_element_type=jnp.float32)
        - drive
    )
    return jnp.maximum(state - rate * slope / scale[None, :], 0.0)


def shards(bricks, brick_coords, brick_counts, step_sizes, init_a, init_b, init_c):
    slab = bricks[0, 0]
    places = brick_coords[0, 0]
    own = brick_counts[0, 0]
    depth = slab.shape[1]
    tile = slab.shape[2]
    sweeps = step_sizes.shape[0]
    state_a = init_a[0]
    state_b = init_b[0]
    state_c = init_c
    for sweep in range(sweeps):
        a_bf = state_a.astype(jnp.bfloat16)
        b_bf = state_b.astype(jnp.bfloat16)
        c_bf = state_c.astype(jnp.bfloat16)
        a_range = lax.all_gather(a_bf, "col", axis=0, tiled=True)
        b_range = lax.all_gather(b_bf, "row", axis=0, tiled=True)
        local_ga = gram(a_bf)
        local_gb = gram(b_bf)
        gram_a, gram_b = lax.psum((local_ga, local_gb), ("row", "col"))
        gram_c = gram(c_bf)

        def own_step(slot, carry):
            total_a, total_b, total_c = carry
            brick = lax.dynamic_index_in_dim(slab, slot, 0, keepdims=False)
            spot = lax.dynamic_index_in_dim(places, slot, 1, keepdims=False)
            i_low = spot[0] * tile
            j_low = spot[1] * tile
            k_low = spot[2] * depth
            a_tile = lax.dynamic_slice_in_dim(a_range, i_low, tile, 0)
            b_tile = lax.dynamic_slice_in_dim(b_range, j_low, tile, 0)
            c_rows = lax.dynamic_slice_in_dim(c_bf, k_low, depth, 0)
            delta_a, delta_b, delta_c = brick_terms(brick, a_tile, b_tile, c_rows)
            return (
                add_tile(total_a, delta_a, i_low),
                add_tile(total_b, delta_b, j_low),
                add_tile(total_c, delta_c, k_low),
            )

        empty = (
            jnp.zeros(a_range.shape, jnp.float32),
            jnp.zeros(b_range.shape, jnp.float32),
            jnp.zeros(c_bf.shape, jnp.float32),
        )
        drive_a, drive_b, drive_c = lax.fori_loop(0, own, own_step, empty)
        mine_a = lax.psum_scatter(drive_a, "col", scatter_dimension=0, tiled=True)
        mine_b = lax.psum_scatter(drive_b, "row", scatter_dimension=0, tiled=True)
        summed_c = lax.psum(drive_c, ("row", "col"))
        new_c = project(state_c, gram_a * gram_b, summed_c, step_sizes[sweep, 2])
        new_a = project(state_a, gram_b * gram_c, mine_a, step_sizes[sweep, 0])
        new_b = project(state_b, gram_a * gram_c, mine_b, step_sizes[sweep, 1])
        state_a, state_b, state_c = (new_a, new_b, new_c)
    return (state_a[None], state_b[None], state_c)


def solution(mesh):
    placed = (
        P("row", "col", None, None, None, None),
        P("row", "col", None, None),
        P("row", "col"),
        P(),
        P("row", "col", None),
        P("col", "row", None),
        P(),
    )
    return jax.shard_map(
        shards,
        mesh=mesh,
        in_specs=placed,
        out_specs=(P("row", "col", None), P("col", "row", None), P()),
        check_vma=False,
    )
```

profile of v0, /device:TPU:17, one launch (start us, length us, event | category | flops | bytes accessed | tf_op | source)
XLA Modules:
  0.0 791.6 jit_solution(12172388770690643116)
XLA Ops:
  8.0 0.0 all-reduce.7.cloned.1.call-start
  8.1 1.7 fusion.61
  9.8 0.7 bitcast_convert_fusion
  10.5 1.7 fusion.59
  12.2 0.7 bitcast_convert_fusion.1
  13.0 31.3 %all_gather.12 = bf16[256,256]{1,0:T(8,128)(2,1)S(1)} all-gather(bf16[16,256]{1,0:T(8,128)(2,1)S(1)} %bitcast_convert_fusion), channel_id=1, replica_groups=mesh['row'=16,'col'=32] {'row'}, dimensions={0}, use_global_device_ids=true | all-gather | bytes 139264 | tf_op jit(solution)/shard_map/all_gather | solution.py:53
  44.3 65.9 %all_gather.13 = bf16[512,256]{1,0:T(8,128)(2,1)S(1)} all-gather(bf16[16,256]{1,0:T(8,128)(2,1)S(1)} %bitcast_convert_fusion.1), channel_id=1, replica_groups=mesh['row'=16,'col'=32] {'col'}, dimensions={0}, use_global_device_ids=true | all-gather | bytes 270336 | tf_op jit(solution)/shard_map/all_gather | solution.py:52
  110.4 6.1 while.28
  111.0 0.6 fusion.93
  113.6 1.7 multiply_reduce_fusion.10
  115.2 0.5 multiply_reduce_fusion.11
  115.7 0.1 add_dynamic-update-slice_fusion.10
  116.5 1.0 copy.16
  117.5 0.0 all-reduce.7.cloned.1.call-update
  117.5 0.0 reduce-scatter.7.cloned.1.call-start
  117.6 0.5 reduce-scatter.7.cloned.1.call-update
  118.1 0.0 reduce-scatter.5.cloned.1.call-start
  118.2 0.5 reduce-scatter.5.cloned.1.call-update
  118.7 0.0 all-reduce.5.cloned.1.call-start
  118.8 0.2 copy.17
  119.0 0.7 fusion.67
  119.6 275.4 %all-reduce.7.cloned.1.call-done = (f32[256,256]{1,0:T(8,128)}, f32[256,256]{1,0:T(8,128)}, f32[512,256]{0,1:T(8,128)}) async-done(((f32[256,256]{1,0:T(8,128)}, f32[256,256]{1,0:T(8,128)}, f32[512,256]{0,1:T(8,128)}), (f32[256,256]{1,0:T(8,128)}, f32[256,256]{1,0:T(8,128)}, f32[512,256]{0,1:T(8,128)})) %all-reduce.7.cloned.1.call-update) | async-done | bytes 1048592 | tf_op jit(solution)/shard_map/psum | solution.py:56
  395.1 1.5 abs_reduce_fusion.3
  396.6 1.7 fusion.69
  398.4 0.1 copy.21
  398.6 0.0 reduce-scatter.7.cloned.1.call-done
  398.6 1.6 fusion.68
  400.2 29.4 %all_gather.14 = bf16[256,256]{1,0:T(8,128)(2,1)S(1)} all-gather(bf16[16,256]{1,0:T(8,128)(2,1)S(1)} %get-tuple-element.215), channel_id=1, replica_groups=mesh['row'=16,'col'=32] {'row'}, dimensions={0}, use_global_device_ids=true | all-gather | bytes 139264 | tf_op jit(solution)/shard_map/all_gather | solution.py:53
  429.6 0.9 fusion.71
  430.5 1.6 fusion.70
  432.1 56.0 %all_gather.15 = bf16[512,256]{1,0:T(8,128)(2,1)S(1)} all-gather(bf16[16,256]{1,0:T(8,128)(2,1)S(1)} %get-tuple-element.219), channel_id=1, replica_groups=mesh['row'=16,'col'=32] {'col'}, dimensions={0}, use_global_device_ids=true | all-gather | bytes 270336 | tf_op jit(solution)/shard_map/all_gather | solution.py:52
  488.1 1.0 fusion.72
  489.2 6.2 while.29
  489.9 0.7 fusion.96
  492.5 1.7 multiply_reduce_fusion.12
  494.2 0.5 multiply_reduce_fusion.13
  494.7 0.1 add_dynamic-update-slice_fusion.12
  495.4 1.0 copy.23
  496.5 0.0 reduce-scatter.11.cloned.1.call-start
  496.5 0.5 reduce-scatter.11.cloned.1.call-update
  497.1 0.0 reduce-scatter.9.cloned.1.call-start
  497.1 0.7 reduce-scatter.9.cloned.1.call-update
  497.8 277.9 %all-reduce.5.cloned.1.call-done = (f32[256,256]{1,0:T(8,128)}, f32[256,256]{1,0:T(8,128)}, f32[512,256]{0,1:T(8,128)}) async-done(((f32[256,256]{1,0:T(8,128)}, f32[256,256]{1,0:T(8,128)}, f32[512,256]{0,1:T(8,128)}), (f32[256,256]{1,0:T(8,128)}, f32[256,256]{1,0:T(8,128)}, f32[512,256]{0,1:T(8,128)})) %all-reduce.5.cloned.1.call-update) | async-done | bytes 1048592 | tf_op jit(solution)/shard_map/psum | solution.py:56
  775.7 1.5 abs_reduce_fusion
  777.3 1.4 fusion.30
  778.7 1.0 copy.25
  779.7 2.2 fusion.35
  781.9 2.1 fusion.40
  (58 shorter events, 0.4 us)
Async XLA Ops:
  8.0 36.3 %copy-start.4 = (f32[512,256]{1,0:T(8,128)S(1)}, f32[512,256]{1,0:T(8,128)}, u32[]{:S(2)}) copy-start(f32[512,256]{1,0:T(8,128)} %param.17) | copy-start | bytes 1572868
  8.0 387.1 %all-reduce.7.cloned.1.call-start = ((), (), s32[]{:S(2)}) async-start(), calls=%async_computation.9 | async-start | bytes 2097152 | tf_op jit(solution)/shard_map/psum | solution.py:56
  44.3 66.1 %copy-start.16 = (s32[1,1,3,2]{2,3,1,0:T(2,128)S(1)}, s32[1,1,3,2]{2,3,1,0:T(2,128)}, u32[]{:S(2)}) copy-start(s32[1,1,3,2]{2,3,1,0:T(2,128)} %param.12) | copy-start | bytes 76
  113.5 1.7 copy-start.13
  116.4 1.1 copy-start.1
  116.4 1.1 copy-start.3
  117.5 1.4 copy-start.12
  117.5 281.0 %reduce-scatter.7.cloned.1.call-start = ((), (), s32[]{:S(2)}) async-start(), calls=%async_computation.5 | async-start | bytes 278528 | tf_op jit(solution)/shard_map/reduce_scatter | solution.py:83
  118.1 312.4 %reduce-scatter.5.cloned.1.call-start = ((), (), s32[]{:S(2)}) async-start(), calls=%async_computation.4 | async-start | bytes 540672 | tf_op jit(solution)/shard_map/reduce_scatter | solution.py:82
  118.7 657.0 %all-reduce.5.cloned.1.call-start = ((), (), s32[]{:S(2)}) async-start(), calls=%async_computation.8 | async-start | bytes 2097152 | tf_op jit(solution)/shard_map/psum | solution.py:56
  395.1 1.5 copy-start.5
  395.1 1.5 copy-start.6
  395.1 1.5 copy-start.9
  396.6 2.0 copy-start.10
  398.4 32.1 %copy-start.11 = (f32[1,16,256]{2,1,0:T(8,128)S(1)}, f32[1,16,256]{2,1,0:T(8,128)}, u32[]{:S(2)}) copy-start(f32[1,16,256]{2,1,0:T(8,128)} %param.15) | copy-start | bytes 49156
  492.5 1.7 copy-start.14
  495.4 1.1 copy-start
  495.4 1.1 copy-start.2
  496.5 283.2 %reduce-scatter.11.cloned.1.call-start = ((), (), s32[]{:S(2)}) async-start(), calls=%async_computation.7 | async-start | bytes 278528 | tf_op jit(solution)/shard_map/reduce_scatter | solution.py:83
  497.1 284.8 %reduce-scatter.9.cloned.1.call-start = ((), (), s32[]{:S(2)}) async-start(), calls=%async_computation.6 | async-start | bytes 540672 | tf_op jit(solution)/shard_map/reduce_scatter | solution.py:82
  775.7 1.5 copy-start.7
  775.7 1.5 copy-start.8
  775.7 1.5 copy-start.15
Sparse Core Ops, SparseCore 0:
  117.6 277.4 all-reduce.6
  496.6 279.0 all-reduce.4
Sparse Core Ops, SparseCore 1:
  120.8 68.2 reduce-scatter.6
  193.5 133.6 reduce-scatter.4
  499.8 69.9 reduce-scatter.10
  574.3 133.7 reduce-scatter.8
where the time goes:
time: 793 us; the launch traced here: 792 us
  waiting for transfers between devices  556 us (70%)
  blocking collectives  183 us (23%)
  matrix products  23.2 us (3%)
  between operations  16 us (2%)
    psum x2, waiting for transfers between devices, shards(): gram_a, gram_b = lax.psum((local_ga, local_gb), ('row', 'col'))  553 us
    all_gather x2, blocking collectives, shards(): a_range = lax.all_gather(a_bf, 'col', axis=0, tiled=True)  122 us
    all_gather x2, blocking collectives, shards(): b_range = lax.all_gather(b_bf, 'row', axis=0, tiled=True)  60.7 us
  transfers between devices with their start and end apart: 6, of which 2 were waited for; matrix products, arithmetic and copies ran while one was open for 2% of the time, Pallas kernels for 0%

commit v1 on v0

--- a/solution.py
+++ b/solution.py
@@ -53,7 +53,7 @@
         b_range = lax.all_gather(b_bf, "row", axis=0, tiled=True)
         local_ga = gram(a_bf)
         local_gb = gram(b_bf)
-        gram_a, gram_b = lax.psum((local_ga, local_gb), ("row", "col"))
+        gram_a, gram_b = lax.psum(lax.psum((local_ga, local_gb), "row"), "col")
         gram_c = gram(c_bf)
 
         def own_step(slot, carry):

time: 793 us -> 2030 us (2.56)
  the two profiles are of different devices: /device:TPU:17 before, /device:TPU:64 now
where the time goes in v1:
time: 2030 us
  waiting for transfers between devices  1790 us (88%)
  blocking collectives  186 us (9%)
  matrix products  25.2 us (1%)
    psum x4, waiting for transfers between devices, shards(): gram_a, gram_b = lax.psum(lax.psum((local_ga, local_gb), 'row'), 'col')  812 us
    psum x2, waiting for transfers between devices, shards(): summed_c = lax.psum(drive_c, ('row', 'col'))  551 us
    reduce_scatter x2, waiting for transfers between devices, shards(): mine_a = lax.psum_scatter(drive_a, 'col', scatter_dimension=0, tiled=True)  259 us
    reduce_scatter x2, waiting for transfers between devices, shards(): mine_b = lax.psum_scatter(drive_b, 'row', scatter_dimension=0, tiled=True)  167 us
    all_gather x2, blocking collectives, shards(): a_range = lax.all_gather(a_bf, 'col', axis=0, tiled=True)  100 us
    all_gather x2, blocking collectives, shards(): b_range = lax.all_gather(b_bf, 'row', axis=0, tiled=True)  86.1 us
  transfers between devices with their start and end apart: 10, of which 10 were waited for; matrix products, arithmetic and copies ran while one was open for 1% of the time, Pallas kernels for 0%

profile of v1, /device:TPU:64, one launch (start us, length us, event | category | flops | bytes accessed | tf_op | source)
XLA Modules:
  0.0 2032.3 jit_solution(9842912187677325405)
XLA Ops:
  7.2 1.7 fusion.61
  9.0 1.7 fusion.59
  10.7 0.0 all-reduce.17.cloned.1.call-start
  10.8 44.0 %all_gather.12 = bf16[256,256]{1,0:T(8,128)(2,1)S(1)} all-gather(bf16[16,256]{1,0:T(8,128)(2,1)S(1)} %bitcast_convert_fusion), channel_id=1, replica_groups=mesh['row'=16,'col'=32] {'row'}, dimensions={0}, use_global_device_ids=true | all-gather | bytes 139264 | tf_op jit(solution)/shard_map/all_gather | solution.py:53
  54.9 50.3 %all_gather.13 = bf16[512,256]{1,0:T(8,128)(2,1)S(1)} all-gather(bf16[16,256]{1,0:T(8,128)(2,1)S(1)} %bitcast_convert_fusion.1), channel_id=1, replica_groups=mesh['row'=16,'col'=32] {'col'}, dimensions={0}, use_global_device_ids=true | all-gather | bytes 270336 | tf_op jit(solution)/shard_map/all_gather | solution.py:52
  105.1 78.4 %all-reduce.21.cloned.1.call-done = (f32[256,256]{1,0:T(8,128)}, f32[256,256]{1,0:T(8,128)}) async-done(((f32[256,256]{1,0:T(8,128)}, f32[256,256]{1,0:T(8,128)}), (f32[256,256]{1,0:T(8,128)}, f32[256,256]{1,0:T(8,128)})) %all-reduce.21.cloned.1.call-update) | async-done | bytes 524304 | tf_op jit(solution)/shard_map/psum | solution.py:56
  183.8 6.2 while.28
  184.5 0.7 fusion.93
  187.1 1.7 multiply_reduce_fusion.10
  188.8 0.4 multiply_reduce_fusion.11
  189.3 0.1 add_dynamic-update-slice_fusion.10
  190.0 0.8 copy-done.1
  190.9 0.5 reduce-scatter.7.cloned.1.call-update
  191.4 1.0 copy.16
  192.5 0.2 copy.17
  192.7 0.4 copy-done.11
  193.1 0.6 fusion.67
  193.7 329.4 %all-reduce.17.cloned.1.call-done = (f32[256,256]{1,0:T(8,128)}, f32[256,256]{1,0:T(8,128)}) async-done(((f32[256,256]{1,0:T(8,128)}, f32[256,256]{1,0:T(8,128)}), (f32[256,256]{1,0:T(8,128)}, f32[256,256]{1,0:T(8,128)})) %all-reduce.17.cloned.1.call-update) | async-done | bytes 524304 | tf_op jit(solution)/shard_map/psum | solution.py:56
  523.1 1.5 abs_reduce_fusion.3
  524.6 135.3 %reduce-scatter.5.cloned.1.call-done = f32[16,256]{1,0:T(8,128)} async-done(((f32[512,256]{1,0:T(8,128)}), f32[16,256]{1,0:T(8,128)}) %reduce-scatter.5.cloned.1.call-update) | async-done | bytes 16400 | tf_op jit(solution)/shard_map/reduce_scatter | solution.py:82
  659.9 1.7 fusion.70
  661.6 83.9 %reduce-scatter.7.cloned.1.call-done = f32[16,256]{1,0:T(8,128)} async-done(((f32[256,256]{1,0:T(8,128)}), f32[16,256]{1,0:T(8,128)}) %reduce-scatter.7.cloned.1.call-update) | async-done | bytes 16400 | tf_op jit(solution)/shard_map/reduce_scatter | solution.py:83
  745.5 1.6 fusion.68
  747.2 0.9 fusion.71
  748.1 0.9 fusion.72
  749.1 269.6 %all-reduce.11.cloned.1.call-done = f32[512,256]{0,1:T(8,128)} async-done(((f32[512,256]{0,1:T(8,128)}), f32[512,256]{0,1:T(8,128)}) %all-reduce.11.cloned.1.call-update) | async-done | bytes 524304 | tf_op jit(solution)/shard_map/psum | solution.py:84
  1018.7 2.8 fusion.69
  1021.5 0.1 copy.21
  1021.6 42.1 %all_gather.14 = bf16[256,256]{1,0:T(8,128)(2,1)S(1)} all-gather(bf16[16,256]{1,0:T(8,128)(2,1)S(1)} %get-tuple-element.217), channel_id=1, replica_groups=mesh['row'=16,'col'=32] {'row'}, dimensions={0}, use_global_device_ids=true | all-gather | bytes 139264 | tf_op jit(solution)/shard_map/all_gather | solution.py:53
  1063.7 50.0 %all_gather.15 = bf16[512,256]{1,0:T(8,128)(2,1)S(1)} all-gather(bf16[16,256]{1,0:T(8,128)(2,1)S(1)} %get-tuple-element.221), channel_id=1, replica_groups=mesh['row'=16,'col'=32] {'col'}, dimensions={0}, use_global_device_ids=true | all-gather | bytes 270336 | tf_op jit(solution)/shard_map/all_gather | solution.py:52
  1113.7 73.6 %all-reduce.19.cloned.1.call-done = (f32[256,256]{1,0:T(8,128)}, f32[256,256]{1,0:T(8,128)}) async-done(((f32[256,256]{1,0:T(8,128)}, f32[256,256]{1,0:T(8,128)}), (f32[256,256]{1,0:T(8,128)}, f32[256,256]{1,0:T(8,128)})) %all-reduce.19.cloned.1.call-update) | async-done | bytes 524304 | tf_op jit(solution)/shard_map/psum | solution.py:56
  1187.4 6.1 while.29
  1188.1 0.6 fusion.96
  1190.6 1.7 multiply_reduce_fusion.12
  1192.3 0.5 multiply_reduce_fusion.13
  1192.8 0.1 add_dynamic-update-slice_fusion.12
  1193.5 1.0 copy.23
  1194.6 0.7 reduce-scatter.9.cloned.1.call-update
  1195.4 0.5 reduce-scatter.11.cloned.1.call-update
  1195.9 330.9 %all-reduce.15.cloned.1.call-done = (f32[256,256]{1,0:T(8,128)}, f32[256,256]{1,0:T(8,128)}) async-done(((f32[256,256]{1,0:T(8,128)}, f32[256,256]{1,0:T(8,128)}), (f32[256,256]{1,0:T(8,128)}, f32[256,256]{1,0:T(8,128)})) %all-reduce.15.cloned.1.call-update) | async-done | bytes 524304 | tf_op jit(solution)/shard_map/psum | solution.py:56
  1526.8 1.5 abs_reduce_fusion
  1528.3 281.8 %all-reduce.13.cloned.1.call-done = f32[512,256]{0,1:T(8,128)} async-done(((f32[512,256]{0,1:T(8,128)}), f32[512,256]{0,1:T(8,128)}) %all-reduce.13.cloned.1.call-update) | async-done | bytes 524304 | tf_op jit(solution)/shard_map/psum | solution.py:84
  1810.1 2.4 fusion.30
  1812.5 1.0 copy.25
  1813.5 124.1 %reduce-scatter.9.cloned.1.call-done = f32[16,256]{1,0:T(8,128)} async-done(((f32[512,256]{1,0:T(8,128)}), f32[16,256]{1,0:T(8,128)}) %reduce-scatter.9.cloned.1.call-update) | async-done | bytes 16400 | tf_op jit(solution)/shard_map/reduce_scatter | solution.py:82
  1937.6 2.2 fusion.40
  1939.8 83.5 %reduce-scatter.11.cloned.1.call-done = f32[16,256]{1,0:T(8,128)} async-done(((f32[256,256]{1,0:T(8,128)}), f32[16,256]{1,0:T(8,128)}) %reduce-scatter.11.cloned.1.call-update) | async-done | bytes 16400 | tf_op jit(solution)/shard_map/reduce_scatter | solution.py:83
  2023.3 2.1 fusion.35
  (66 shorter events, 0.9 us)
Async XLA Ops:
  7.2 3.6 copy-start.10
  7.2 47.7 %copy-start.9 = (f32[1,16,256]{2,1,0:T(8,128)S(1)}, f32[1,16,256]{2,1,0:T(8,128)}, u32[]{:S(2)}) copy-start(f32[1,16,256]{2,1,0:T(8,128)} %param.15) | copy-start | bytes 49156
  7.2 3.6 copy-start.4
  7.2 176.4 %all-reduce.21.cloned.1.call-start = ((), (), s32[]{:S(2)}) async-start(), calls=%async_computation.13 | async-start | bytes 1048576 | tf_op jit(solution)/shard_map/psum | solution.py:56
  10.7 512.4 %all-reduce.17.cloned.1.call-start = ((), (), s32[]{:S(2)}) async-start(), calls=%async_computation.11 | async-start | bytes 1048576 | tf_op jit(solution)/shard_map/psum | solution.py:56
  54.9 128.9 %copy-start.14 = (s32[1,1,3,2]{2,3,1,0:T(2,128)S(1)}, s32[1,1,3,2]{2,3,1,0:T(2,128)}, u32[]{:S(2)}) copy-start(s32[1,1,3,2]{2,3,1,0:T(2,128)} %param.12) | copy-start | bytes 76
  183.6 476.3 %reduce-scatter.5.cloned.1.call-start = ((), (), s32[]{:S(2)}) async-start(), calls=%async_computation.4 | async-start | bytes 540672 | tf_op jit(solution)/shard_map/reduce_scatter | solution.py:82
  187.1 1.7 copy-start.12
  190.0 0.8 copy-start.1
  190.0 0.9 copy-start.3
  190.8 554.7 %reduce-scatter.7.cloned.1.call-start = ((), (), s32[]{:S(2)}) async-start(), calls=%async_computation.5 | async-start | bytes 278528 | tf_op jit(solution)/shard_map/reduce_scatter | solution.py:83
  191.4 827.3 %all-reduce.11.cloned.1.call-start = ((), (), s32[]{:S(2)}) async-start(), calls=%async_computation.6 | async-start | bytes 1048576 | tf_op jit(solution)/shard_map/psum | solution.py:84
  192.4 0.7 copy-start.11
  192.5 994.8 %all-reduce.19.cloned.1.call-start = ((), (), s32[]{:S(2)}) async-start(), calls=%async_computation.12 | async-start | bytes 1048576 | tf_op jit(solution)/shard_map/psum | solution.py:56
  523.1 136.8 %copy-start.5 = (f32[256,256]{1,0:T(8,128)S(1)}, f32[256,256]{1,0:T(8,128)}, u32[]{:S(2)}) copy-start(f32[256,256]{1,0:T(8,128)} %get-tuple-element.194) | copy-start | bytes 786436
  523.1 222.4 %copy-start.6 = (f32[256,256]{1,0:T(8,128)S(1)}, f32[256,256]{1,0:T(8,128)}, u32[]{:S(2)}) copy-start(f32[256,256]{1,0:T(8,128)} %get-tuple-element.195) | copy-start | bytes 786436
  749.0 777.8 %all-reduce.15.cloned.1.call-start = ((), (), s32[]{:S(2)}) async-start(), calls=%async_computation.10 | async-start | bytes 1048576 | tf_op jit(solution)/shard_map/psum | solution.py:56
  1187.3 622.8 %all-reduce.13.cloned.1.call-start = ((), (), s32[]{:S(2)}) async-start(), calls=%async_computation.9 | async-start | bytes 1048576 | tf_op jit(solution)/shard_map/psum | solution.py:84
  1190.6 1.7 copy-start.13
  1193.5 1.1 copy-start
  1193.5 1.8 copy-start.2
  1194.6 743.1 %reduce-scatter.9.cloned.1.call-start = ((), (), s32[]{:S(2)}) async-start(), calls=%async_computation.7 | async-start | bytes 540672 | tf_op jit(solution)/shard_map/reduce_scatter | solution.py:82
  1195.3 828.0 %reduce-scatter.11.cloned.1.call-start = ((), (), s32[]{:S(2)}) async-start(), calls=%async_computation.8 | async-start | bytes 278528 | tf_op jit(solution)/shard_map/reduce_scatter | solution.py:83
  1526.8 283.3 %copy-start.7 = (f32[256,256]{1,0:T(8,128)S(1)}, f32[256,256]{1,0:T(8,128)}, u32[]{:S(2)}) copy-start(f32[256,256]{1,0:T(8,128)} %get-tuple-element.193) | copy-start | bytes 786436
  1526.8 283.3 %copy-start.8 = (f32[256,256]{1,0:T(8,128)S(1)}, f32[256,256]{1,0:T(8,128)}, u32[]{:S(2)}) copy-start(f32[256,256]{1,0:T(8,128)} %get-tuple-element.192) | copy-start | bytes 786436
Sparse Core Ops, SparseCore 0:
  11.5 172.0 all-reduce.20
  186.5 336.5 all-reduce.16
  528.3 131.5 reduce-scatter.4
  662.6 82.9 reduce-scatter.6
  750.4 268.2 all-reduce.10
  1022.1 165.1 all-reduce.18
  1190.2 336.5 all-reduce.14
  1532.4 277.6 all-reduce.12
  1814.7 122.8 reduce-scatter.8
  1940.3 82.9 reduce-scatter.10
